TPU v7x, 256 devices: a whole 4x4x8 slice. The times are simulated.
256 devices in a mesh: dp: 16 (over y_lo, x, core), seq: 16 (over z, y_hi).
Axes of the slice: x: 4, y: 4 (y_hi: 2, y_lo: 2; y = y_hi * 2 + y_lo), z: 8, core: 2. Of those that a mesh axis runs over, the one named last changes fastest.
Arguments:
- student_in: bfloat16 [32768, 3584], P(('dp', 'seq')), may hold values from -24 to 24
- weight: bfloat16 [3584, 512], P(('dp', 'seq')), may hold values from -0.09375 to 0.09375
- queries: bfloat16 [32768, 512], P(('dp', 'seq')), may hold values from -8 to 8, as said below
- keys: bfloat16 [32768, 128], P(('dp', 'seq')), may hold values from -8 to 8
- values: bfloat16 [32768, 128], P(('dp', 'seq')), may hold values from -6 to 6
- lengths: int32 [16, 4], P('dp'), may hold values from 1 to 1536, 2048 in all within a row
- assignment: int32 [16, 16], P('dp'), may hold values from 0 to 15, each once within a row
Outputs:
- attention: bfloat16 [32768, 512], P(('dp', 'seq'))
- weight_grad: float32 [3584, 512], P(('dp', 'seq'))
Inputs may be any that keep to these rules, and one draw needn't show every extreme that they name: `queries`: entries of head 0 and of keys may reach the ends of this range. Each row holds the lengths of 4 rollouts of one sequence, summing to 2048, the longest exactly 1536. `assignment`: each row is a permutation of the 16 rollout blocks of one sequence.
All inputs are finite; a program needn't handle non-finite values.
Results may differ from a plain program's by a relative error of at most 0.012.
Values may be sent and summed in bfloat16 or wider, within the bound.
No kernel may reach another device: no remote copies, remote signals or barrier semaphores. Data moves between devices by JAX's collectives and lax.ppermute only.
A program may use at most 64 MiB of HBM per device.

v0:
```python
import math
import jax
import jax.numpy as jnp
from jax import lax
from jax.sharding import PartitionSpec as P

HD = 128
HQ = 4
BLK = 128
EPSILON = 1e-06
NEGATIVE = -1e30


def side_by_side(arrays, axis, dim, along):
    both = jnp.concatenate(arrays, axis=along)
    whole, at, gathered = (lax.all_gather(both, axis, axis=dim, tiled=True), 0, [])
    for a in arrays:
        gathered.append(lax.slice_in_dim(whole, at, at + a.shape[along], axis=along))
        at += a.shape[along]
    return tuple(gathered)


def laid_out(tiles, dim):
    tiles = jnp.moveaxis(tiles, 0, dim)
    dims = tiles.shape
    return tiles.reshape(*dims[:dim], dims[dim] * dims[dim + 1], *dims[dim + 2 :])


def from_everyone(x, axis):
    copies = jnp.broadcast_to(x, (lax.axis_size(axis), *x.shape))
    return lax.all_to_all(copies, axis, split_axis=0, concat_axis=0, tiled=True)


def collect(x, axis, dim):
    return laid_out(from_everyone(x, axis), dim)


def in_blocks(x, dim, length):
    before, after = (x.shape[:dim], x.shape[dim + 1 :])
    return jnp.moveaxis(x.reshape(*before, length, -1, *after), dim, 0)


def sum_at_owner(x, axis, dim):
    tiles = in_blocks(x, dim, lax.axis_size(axis))
    arrived = lax.all_to_all(tiles, axis, split_axis=0, concat_axis=0, tiled=True)
    return arrived.astype(jnp.float32).sum(axis=0)


def locate(assign_row, doc_ends, first_slot, count):
    slot_ids = first_slot + jnp.arange(count, dtype=jnp.int32)
    block_ids = slot_ids // BLK
    block_table = jnp.arange(assign_row.shape[0], dtype=jnp.int32)
    placed = jnp.sum(
        jnp.where(block_ids[:, None] == block_table[None, :], assign_row[None, :], 0), axis=1
    )
    position = placed * BLK + slot_ids % BLK
    document = jnp.sum((position[:, None] >= doc_ends[None, :]).astype(jnp.int32), axis=1)
    return (position, document)


def absorb_block(state, key_block, value_block, query_heads, allowed):
    run_max, run_total, run_acc = state
    scores = jnp.einsum(
        "qhd,kd->hqk", query_heads, key_block, preferred_element_type=jnp.float32
    ) * HD ** (-0.5)
    masked = jnp.where(allowed[None], scores, NEGATIVE)
    new_max = jnp.maximum(run_max, jnp.max(masked, axis=-1))
    fading = jnp.exp(run_max - new_max)
    exp_terms = jnp.where(allowed[None], jnp.exp(masked - new_max[:, :, None]), 0.0)
    new_total = run_total * fading + jnp.sum(exp_terms, axis=-1)
    mixture = jnp.einsum(
        "hqk,kd->qhd",
        exp_terms.astype(jnp.bfloat16),
        value_block,
        preferred_element_type=jnp.float32,
    )
    new_acc = run_acc * fading.T[:, :, None] + mixture
    return (new_max, new_total, new_acc)


def local(student_in, weight, queries, keys, values, lengths, assignment):
    rows = queries.shape[0]
    assign_row = assignment[0]
    doc_ends = jnp.cumsum(lengths[0])
    query_pos, query_doc = locate(assign_row, doc_ends, lax.axis_index("seq") * rows, rows)
    query_heads = queries.reshape(rows, HQ, HD)
    start_state = (
        jnp.full((HQ, rows), NEGATIVE, jnp.float32),
        jnp.zeros((HQ, rows), jnp.float32),
        jnp.zeros((rows, HQ, HD), jnp.float32),
    )
    key_piece, value_piece = side_by_side((keys, values), "seq", 0, 1)
    count = key_piece.shape[0]
    step_rows = math.gcd(count, 512)
    steps_count = count // step_rows
    key_pos, key_doc = locate(assign_row, doc_ends, jnp.int32(0), count)

    def one_step(running, slabs):
        key_block, value_block, key_position, key_document = slabs
        allowed = (query_doc[:, None] == key_document[None, :]) & (
            query_pos[:, None] >= key_position[None, :]
        )
        updated = absorb_block(running, key_block, value_block, query_heads, allowed)
        return (updated, None)

    slabs = (
        key_piece.reshape(steps_count, step_rows, HD),
        value_piece.reshape(steps_count, step_rows, HD),
        key_pos.reshape(steps_count, step_rows),
        key_doc.reshape(steps_count, step_rows),
    )
    result, _ = lax.scan(one_step, start_state, slabs)
    final_max, final_total, final_acc = result
    attention = (final_acc / final_total.T[:, :, None]).reshape(rows, HQ * HD).astype(jnp.bfloat16)
    as_float = student_in.astype(jnp.float32)
    normed = (
        as_float * lax.rsqrt(jnp.mean(as_float * as_float, axis=1, keepdims=True) + EPSILON)
    ).astype(jnp.bfloat16)
    group_rows = collect(weight, "seq", 0)
    columns = normed
    predicted = jnp.dot(
        columns,
        lax.all_gather(group_rows, "dp", axis=0, tiled=True),
        preferred_element_type=jnp.float32,
    )
    dp_count = lax.axis_size("dp")
    seq_count = lax.axis_size("seq")
    token_total = rows * dp_count * seq_count
    scaled = ((predicted - attention.astype(jnp.float32)) * token_total ** (-0.5)).astype(
        jnp.bfloat16
    )
    columns = normed
    outer_rows = lax.psum_scatter(
        lax.dot_general(
            columns, scaled, (((0,), (0,)), ((), ())), preferred_element_type=jnp.float32
        ).astype(jnp.bfloat16),
        "dp",
        scatter_dimension=0,
        tiled=True,
    )
    weight_grad = sum_at_owner(outer_rows, "seq", 0)
    return (attention, weight_grad)


def solution(mesh):
    placed = (
        P(("dp", "seq"), None),
        P(("dp", "seq"), None),
        P(("dp", "seq"), None),
        P(("dp", "seq"), None),
        P(("dp", "seq"), None),
        P("dp", None),
        P("dp", None),
    )
    return jax.shard_map(
        local,
        mesh=mesh,
        in_specs=placed,
        out_specs=(P(("dp", "seq"), None), P(("dp", "seq"), None)),
        check_vma=False,
    )
```

profile of v0, /device:TPU:7, one launch (start us, length us, event | category | flops | bytes accessed | tf_op | source)
XLA Modules:
  0.0 233.3 jit_solution(15278113678716373417)
XLA Ops:
  7.2 0.0 all-gather.3.cloned.1.call-start
  7.2 1.4 pad_maximum_fusion
  8.6 0.0 all-gather.3.cloned.1.call-update
  8.6 1.4 broadcast_in_dim.82
  10.1 10.9 %all-to-all-start = ((bf16[16,14,512]{2,1,0:T(8,128)(2,1)}), bf16[16,14,512]{2,1,0:T(8,128)(2,1)S(1)}, u32[]{:S(2)}, u32[]{:S(2)}) async-start(bf16[16,14,512]{2,1,0:T(8,128)(2,1)} %broadcast_in_dim.82), calls=%async_computation | async-start | bytes 524288 | tf_op jit(solution)/shard_map/all_to_all | solution.py:31
  21.0 0.0 all-gather.5.cloned.1.call-start
  21.1 0.8 reduce-window.8
  21.9 0.7 select_reduce_fusion.1
  22.7 0.8 select_reduce_fusion
  23.4 0.1 convert_reduce_fusion.1
  23.5 0.1 convert_reduce_fusion.2
  23.7 1.0 copy.17
  24.7 0.1 copy.18
  24.8 1.5 fusion.18
  26.3 6.7 %all-to-all-done = bf16[16,14,512]{2,1,0:T(8,128)(2,1)S(1)} async-done(((bf16[16,14,512]{2,1,0:T(8,128)(2,1)}), bf16[16,14,512]{2,1,0:T(8,128)(2,1)S(1)}, u32[]{:S(2)}, u32[]{:S(2)}) %all-to-all-start) | async-done | bytes 229408 | tf_op jit(solution)/shard_map/all_to_all | solution.py:31
  33.0 0.8 reshape.189
  33.8 0.0 all-gather.5.cloned.1.call-update
  33.8 0.0 reduce-scatter.2.cloned.1.call-start
  33.9 55.3 %all-gather.3.cloned.1.call-done = bf16[2048,256]{1,0:T(8,128)(2,1)} async-done(((bf16[128,256]{1,0:T(8,128)(2,1)}), bf16[2048,256]{1,0:T(8,128)(2,1)}) %all-gather.3.cloned.1.call-update) | async-done | bytes 1048592 | tf_op jit(solution)/shard_map/all_gather | solution.py:16
  89.2 1.3 fusion.41
  90.5 0.0 copy-start
  90.5 4.8 %while.15 = (s32[]{:T(128)}, f32[4,128]{1,0:T(4,128)S(1)}, f32[4,128]{1,0:T(4,128)S(1)}, f32[128,4,128]{0,2,1:T(8,128)S(1)}, s32[128]{0:T(128)S(1)}, /*index=5*/...) while((s32[]{:T(128)}, f32[4,128]{1,0:T(4,128)S(1)}, ...), condition=%wide.region_8.9_spmd.clone, body=%wide.region_5.8_spmd.clone.sunk | while | flops 136973312 | bytes 4371613 | solution.py:112
  90.5 0.2 compare_and_fusion.2
  90.7 0.3 fusion.55
  91.1 0.2 fusion.57
  91.3 0.4 fusion.59
  91.7 0.2 compare_and_fusion.2
  91.9 0.3 fusion.55
  92.2 0.2 fusion.57
  92.5 0.4 fusion.59
  92.9 0.2 compare_and_fusion.2
  93.1 0.3 fusion.55
  93.4 0.2 fusion.57
  93.7 0.4 fusion.59
  94.1 0.2 compare_and_fusion.2
  94.3 0.3 fusion.55
  94.6 0.2 fusion.57
  94.8 0.4 fusion.59
  95.3 0.1 copy.22
  95.4 0.0 copy-start.1
  95.4 34.6 %all-gather.5.cloned.1.call-done = bf16[3584,512]{1,0:T(8,128)(2,1)} async-done(((bf16[224,512]{1,0:T(8,128)(2,1)}), bf16[3584,512]{1,0:T(8,128)(2,1)}) %all-gather.5.cloned.1.call-update) | async-done | bytes 3670032 | tf_op jit(solution)/shard_map/all_gather | solution.py:123
  130.1 0.0 copy-done
  130.1 5.7 %convolution_convert_fusion = bf16[3584,512]{1,0:T(8,128)(2,1)} fusion(bf16[3584,512]{1,0:T(8,128)(2,1)} %all-gather.5.cloned.1.call-done, bf16[128,3584]{1,0:T(8,128)(2,1)S(1)} %copy-done, f32[128]{0:T(128)S(1)} %add_rsqrt_fusion, bf16[128,512]{1,0:T(8,128)(2,1)S(1)} %copy.22), kind=kOutput, calls=%fused_computation.27 | convolution fusion | flops 944373760 | bytes 8389120 | tf_op jit(solution)/shard_map/dot_general | solution.py:134
  135.7 0.0 reduce-scatter.2.cloned.1.call-update
  135.8 67.5 %reduce-scatter.2.cloned.1.call-done = bf16[224,512]{1,0:T(8,128)(2,1)} async-done(((bf16[3584,512]{1,0:T(8,128)(2,1)}), bf16[224,512]{1,0:T(8,128)(2,1)}) %reduce-scatter.2.cloned.1.call-update) | async-done | bytes 229392 | tf_op jit(solution)/shard_map/reduce_scatter | solution.py:133
  203.2 1.0 reshape.190
  204.3 21.9 %all_to_all.10 = bf16[16,14,512]{2,1,0:T(8,128)(2,1)S(1)} all-to-all(bf16[16,14,512]{2,1,0:T(8,128)(2,1)S(1)} %reshape.190), channel_id=1, replica_groups=mesh['dp'=16,'seq'=16] {'seq'}, dimensions={0} | all-to-all | bytes 458752 | tf_op jit(solution)/shard_map/all_to_all | solution.py:45
  226.1 0.7 convert_reduce_fusion
  (29 shorter events, 0.3 us)
Async XLA Ops:
  7.2 82.0 %all-gather.3.cloned.1.call-start = ((), (), s32[]{:S(2)}) async-start(), calls=%async_computation.3 | async-start | bytes 1114112 | tf_op jit(solution)/shard_map/all_gather | solution.py:16
  10.1 22.9 %all-to-all-start = ((bf16[16,14,512]{2,1,0:T(8,128)(2,1)}), bf16[16,14,512]{2,1,0:T(8,128)(2,1)S(1)}, u32[]{:S(2)}, u32[]{:S(2)}) async-start(bf16[16,14,512]{2,1,0:T(8,128)(2,1)} %broadcast_in_dim.82), calls=%async_computation | async-start | bytes 524288 | tf_op jit(solution)/shard_map/all_to_all | solution.py:31
  21.0 109.1 %all-gather.5.cloned.1.call-start = ((), (), s32[]{:S(2)}) async-start(), calls=%async_computation.4 | async-start | bytes 3899392 | tf_op jit(solution)/shard_map/all_gather | solution.py:123
  33.8 169.4 %reduce-scatter.2.cloned.1.call-start = ((), (), s32[]{:S(2)}) async-start(), calls=%async_computation.5 | async-start | bytes 3899392 | tf_op jit(solution)/shard_map/reduce_scatter | solution.py:133
  90.5 39.6 %copy-start = (bf16[128,3584]{1,0:T(8,128)(2,1)S(1)}, bf16[128,3584]{1,0:T(8,128)(2,1)}, u32[]{:S(2)}) copy-start(bf16[128,3584]{1,0:T(8,128)(2,1)} %param.9) | copy-start | bytes 2752516
  95.4 40.3 %copy-start.1 = (bf16[128,512]{1,0:T(8,128)(2,1)}, bf16[128,512]{1,0:T(8,128)(2,1)S(1)}, u32[]{:S(2)}) copy-start(bf16[128,512]{1,0:T(8,128)(2,1)S(1)} %copy.22) | copy-start | bytes 393220
Sparse Core Ops, SparseCore 0:
  11.2 77.9 all-gather.2
  91.0 38.9 all-gather.4
  135.9 67.3 reduce-scatter.1
where the time goes:
time: 234 us; the launch traced here: 233 us
  waiting for transfers between devices  164 us (70%)
  blocking collectives  21.9 us (9%)
  between operations  13.9 us (6%)
  starting transfers between devices  11 us (5%)
  matrix products  8.39 us (4%)
  other arithmetic  7.86 us (3%)
  local copies, waits for them, and re-layouts  5.83 us (2%)
    reduce_scatter x1, waiting for transfers between devices, local(): lax.psum_scatter(lax.dot_general(columns, scaled, (((0,), (0,)), ((), ())...  67.5 us
    all_gather x1, waiting for transfers between devices, side_by_side(): lax.all_gather(both, axis, axis=dim, tiled=True)  55.3 us
    all_gather x1, waiting for transfers between devices, local(): lax.all_gather(group_rows, 'dp', axis=0, tiled=True)  34.6 us
    all_to_all x1, blocking collectives, sum_at_owner(): lax.all_to_all(tiles, axis, split_axis=0, concat_axis=0, tiled=True)  21.9 us
    all_to_all x1, starting transfers between devices, from_everyone(): return lax.all_to_all(copies, axis, split_axis=0, concat_axis=0, tiled=True)  10.9 us
    all_to_all x1, waiting for transfers between devices, from_everyone(): return lax.all_to_all(copies, axis, split_axis=0, concat_axis=0, tiled=True)  6.72 us
    dot_general x1, matrix products, local(): lax.dot_general(columns, scaled, (((0,), (0,)), ((), ())), preferred_elem...  5.65 us
  transfers between devices with their start and end apart: 4, of which 4 were waited for; matrix products, arithmetic and copies ran while one was open for 6% of the time, Pallas kernels for 0%

commit v1 on v0

--- a/solution.py
+++ b/solution.py
@@ -120,7 +120,9 @@
     columns = normed
     predicted = jnp.dot(
         columns,
-        lax.all_gather(group_rows, "dp", axis=0, tiled=True),
+        jnp.concatenate(
+            lax.all_to_all(jnp.stack([group_rows] * lax.axis_size("dp")), "dp", 0, 0), axis=0
+        ),
         preferred_element_type=jnp.float32,
     )
     dp_count = lax.axis_size("dp")

time: 234 us -> 216 us (0.923)
  waiting for transfers between devices: 164 us -> 137 us
  starting transfers between devices: 11 us -> 18 us
    all_gather x1 -> x0, waiting for transfers between devices: 34.6 us -> none  [local(): lax.all_gather(group_rows, 'dp', axis=0, tiled=True)]
    all_to_all x0 -> x1, starting transfers between devices: none -> 7.04 us  [local(): lax.all_to_all(jnp.stack([group_rows] * lax.axis_size('dp')), 'dp', 0, 0)]
    all_gather x1, waiting for transfers between devices: 55.3 us -> 61.3 us  [side_by_side(): lax.all_gather(both, axis, axis=dim, tiled=True)]
  transfers between devices with their start and end apart: 4 -> 4, of which waited for: 4 -> 3; matrix products, arithmetic and copies ran while one was open for 6% -> 7% of each run, Pallas kernels for 0% -> 0%
where the time goes in v1:
time: 216 us; the launch traced here: 215 us
  waiting for transfers between devices  137 us (63%)
  blocking collectives  21.9 us (10%)
  starting transfers between devices  18 us (8%)
  between operations  14.2 us (7%)
  matrix products  8.41 us (4%)
  other arithmetic  7.86 us (4%)
  local copies, waits for them, and re-layouts  7.33 us (3%)
    reduce_scatter x1, waiting for transfers between devices, local(): lax.psum_scatter(lax.dot_general(columns, scaled, (((0,), (0,)), ((), ())...  69.2 us
    all_gather x1, waiting for transfers between devices, side_by_side(): lax.all_gather(both, axis, axis=dim, tiled=True)  61.3 us
    all_to_all x1, blocking collectives, sum_at_owner(): lax.all_to_all(tiles, axis, split_axis=0, concat_axis=0, tiled=True)  21.9 us
    all_to_all x1, starting transfers between devices, from_everyone(): return lax.all_to_all(copies, axis, split_axis=0, concat_axis=0, tiled=True)  10.9 us
    all_to_all x1, starting transfers between devices, local(): lax.all_to_all(jnp.stack([group_rows] * lax.axis_size('dp')), 'dp', 0, 0)  7.04 us
    all_to_all x1, waiting for transfers between devices, from_everyone(): return lax.all_to_all(copies, axis, split_axis=0, concat_axis=0, tiled=True)  6.74 us
    dot_general x1, matrix products, local(): lax.dot_general(columns, scaled, (((0,), (0,)), ((), ())), preferred_elem...  5.7 us
  transfers between devices with their start and end apart: 4, of which 3 were waited for; matrix products, arithmetic and copies ran while one was open for 7% of the time, Pallas kernels for 0%

profile of v1, /device:TPU:7, one launch (start us, length us, event | category | flops | bytes accessed | tf_op | source)
XLA Modules:
  0.0 215.3 jit_solution(4083643474519896397)
XLA Ops:
  7.2 0.0 all-gather.2.cloned.1.call-start
  7.2 1.4 pad_maximum_fusion
  8.6 0.0 all-gather.2.cloned.1.call-update
  8.6 1.4 broadcast_in_dim.82
  10.1 10.9 %all-to-all-start = ((bf16[16,14,512]{2,1,0:T(8,128)(2,1)}), bf16[16,14,512]{2,1,0:T(8,128)(2,1)S(1)}, u32[]{:S(2)}, u32[]{:S(2)}) async-start(bf16[16,14,512]{2,1,0:T(8,128)(2,1)} %broadcast_in_dim.82), calls=%async_computation | async-start | bytes 524288 | tf_op jit(solution)/shard_map/all_to_all | solution.py:31
  21.0 0.8 reduce-window.8
  21.9 0.8 select_reduce_fusion
  22.6 0.1 convert_reduce_fusion.1
  22.8 1.0 copy.17
  23.8 0.1 copy.18
  24.0 0.7 select_reduce_fusion.1
  24.7 0.1 convert_reduce_fusion.2
  24.8 1.4 fusion.18
  26.3 6.7 %all-to-all-done = bf16[16,14,512]{2,1,0:T(8,128)(2,1)S(1)} async-done(((bf16[16,14,512]{2,1,0:T(8,128)(2,1)}), bf16[16,14,512]{2,1,0:T(8,128)(2,1)S(1)}, u32[]{:S(2)}, u32[]{:S(2)}) %all-to-all-start) | async-done | bytes 229408 | tf_op jit(solution)/shard_map/all_to_all | solution.py:31
  33.0 0.1 stack_reshape.2
  33.1 2.2 %stack.3 = bf16[16,224,512]{2,1,0:T(8,128)(2,1)} broadcast(bf16[224,512]{1,0:T(8,128)(2,1)S(1)} %stack_reshape.2), dimensions={1,2} | broadcast | bytes 3899392 | tf_op jit(solution)/shard_map/stack | solution.py:124
  35.3 7.0 %all-to-all-start.1 = ((bf16[16,224,512]{2,1,0:T(8,128)(2,1)}), bf16[16,224,512]{2,1,0:T(8,128)(2,1)}, u32[]{:S(2)}, u32[]{:S(2)}) async-start(bf16[16,224,512]{2,1,0:T(8,128)(2,1)} %stack.3), calls=%async_computation.1 | async-start | bytes 7340032 | tf_op jit(solution)/shard_map/all_to_all | solution.py:124
  42.3 0.0 reduce-scatter.2.cloned.1.call-start
  42.4 61.3 %all-gather.2.cloned.1.call-done = bf16[2048,256]{1,0:T(8,128)(2,1)} async-done(((bf16[128,256]{1,0:T(8,128)(2,1)}), bf16[2048,256]{1,0:T(8,128)(2,1)}) %all-gather.2.cloned.1.call-update) | async-done | bytes 1048592 | tf_op jit(solution)/shard_map/all_gather | solution.py:16
  103.7 1.3 fusion.41
  105.0 0.0 copy-start
  105.0 4.8 %while.15 = (s32[]{:T(128)}, f32[4,128]{1,0:T(4,128)S(1)}, f32[4,128]{1,0:T(4,128)S(1)}, f32[128,4,128]{0,2,1:T(8,128)S(1)}, s32[128]{0:T(128)S(1)}, /*index=5*/...) while((s32[]{:T(128)}, f32[4,128]{1,0:T(4,128)S(1)}, ...), condition=%wide.region_8.9_spmd.clone, body=%wide.region_5.8_spmd.clone.sunk | while | flops 136973312 | bytes 4371605 | solution.py:112
  105.0 0.2 compare_and_fusion.2
  105.2 0.3 fusion.55
  105.5 0.4 fusion.59
  105.9 0.2 fusion.57
  106.2 0.2 compare_and_fusion.2
  106.4 0.3 fusion.55
  106.7 0.4 fusion.59
  107.1 0.2 fusion.57
  107.4 0.2 compare_and_fusion.2
  107.6 0.3 fusion.55
  107.9 0.4 fusion.59
  108.3 0.2 fusion.57
  108.6 0.2 compare_and_fusion.2
  108.8 0.3 fusion.55
  109.1 0.4 fusion.59
  109.5 0.2 fusion.57
  109.8 0.1 copy.22
  109.9 0.0 copy-start.1
  109.9 0.0 all-to-all-done.1
  109.9 0.0 copy-done
  109.9 5.7 %convolution_convert_fusion = bf16[3584,512]{1,0:T(8,128)(2,1)} fusion(bf16[3584,512]{1,0:T(8,128)(2,1)} %bitcast.8, bf16[128,3584]{1,0:T(8,128)(2,1)S(1)} %copy-done, f32[128]{0:T(128)S(1)} %add_rsqrt_fusion, bf16[128,512]{1,0:T(8,128)(2,1)S(1)} %copy.22), kind=kOutput, calls=%fused_computation.27 | convolution fusion | flops 944373760 | bytes 8389120 | tf_op jit(solution)/shard_map/dot_general | solution.py:136
  115.6 0.0 reduce-scatter.2.cloned.1.call-update
  115.7 69.2 %reduce-scatter.2.cloned.1.call-done = bf16[224,512]{1,0:T(8,128)(2,1)} async-done(((bf16[3584,512]{1,0:T(8,128)(2,1)}), bf16[224,512]{1,0:T(8,128)(2,1)}) %reduce-scatter.2.cloned.1.call-update) | async-done | bytes 229392 | tf_op jit(solution)/shard_map/reduce_scatter | solution.py:135
  184.8 1.0 reshape.192
  185.8 21.9 %all_to_all.15 = bf16[16,14,512]{2,1,0:T(8,128)(2,1)S(1)} all-to-all(bf16[16,14,512]{2,1,0:T(8,128)(2,1)S(1)} %reshape.192), channel_id=1, replica_groups=mesh['dp'=16,'seq'=16] {'seq'}, dimensions={0} | all-to-all | bytes 458752 | tf_op jit(solution)/shard_map/all_to_all | solution.py:45
  207.8 0.7 convert_reduce_fusion
  (29 shorter events, 0.3 us)
Async XLA Ops:
  7.2 96.5 %all-gather.2.cloned.1.call-start = ((), (), s32[]{:S(2)}) async-start(), calls=%async_computation.4 | async-start | bytes 1114112 | tf_op jit(solution)/shard_map/all_gather | solution.py:16
  10.1 22.9 %all-to-all-start = ((bf16[16,14,512]{2,1,0:T(8,128)(2,1)}), bf16[16,14,512]{2,1,0:T(8,128)(2,1)S(1)}, u32[]{:S(2)}, u32[]{:S(2)}) async-start(bf16[16,14,512]{2,1,0:T(8,128)(2,1)} %broadcast_in_dim.82), calls=%async_computation | async-start | bytes 524288 | tf_op jit(solution)/shard_map/all_to_all | solution.py:31
  35.3 74.6 %all-to-all-start.1 = ((bf16[16,224,512]{2,1,0:T(8,128)(2,1)}), bf16[16,224,512]{2,1,0:T(8,128)(2,1)}, u32[]{:S(2)}, u32[]{:S(2)}) async-start(bf16[16,224,512]{2,1,0:T(8,128)(2,1)} %stack.3), calls=%async_computation.1 | async-start | bytes 7340032 | tf_op jit(solution)/shard_map/all_to_all | solution.py:124
  42.3 142.5 %reduce-scatter.2.cloned.1.call-start = ((), (), s32[]{:S(2)}) async-start(), calls=%async_computation.5 | async-start | bytes 3899392 | tf_op jit(solution)/shard_map/reduce_scatter | solution.py:135
  105.0 5.0 %copy-start = (bf16[128,3584]{1,0:T(8,128)(2,1)S(1)}, bf16[128,3584]{1,0:T(8,128)(2,1)}, u32[]{:S(2)}) copy-start(bf16[128,3584]{1,0:T(8,128)(2,1)} %param.9) | copy-start | bytes 2752516
  109.9 5.7 %copy-start.1 = (bf16[128,512]{1,0:T(8,128)(2,1)}, bf16[128,512]{1,0:T(8,128)(2,1)S(1)}, u32[]{:S(2)}) copy-start(bf16[128,512]{1,0:T(8,128)(2,1)S(1)} %copy.22) | copy-start | bytes 393220
Sparse Core Ops, SparseCore 0:
  11.2 92.4 all-gather.1
  115.8 68.9 reduce-scatter.1
